TPU v7x, 32 devices: a whole 2x2x4 slice. The times are simulated.
32 devices in a mesh: scene: 2 (over x), pulse: 16 (over z, y, core).
Axes of the slice: x: 2, y: 2, z: 4, core: 2. Of those that a mesh axis runs over, the one named last changes fastest.
Arguments:
- beams: bfloat16 [2, 2048, 4096], P(None, ('scene', 'pulse')), parts along dimension 1, may hold values from -6 to 6
- ukern: bfloat16 [2, 32], replicated, may hold values from -1 to 1
- rkern: float32 [16, 4], replicated, may hold values from -3 to 3
- angles: float32 [4, 2, 128], replicated, may hold values from -3.140625 to 3.140625
- taps: int32 [4, 2048], P(None, ('scene', 'pulse')), parts along dimension 1, may hold values from 0 to 15
- shifts: int32 [4, 16], replicated, may hold values from -48 to 48
- half_table: int32 [4, 16], replicated, may hold values from 0 to 1, as said below
Outputs:
- merged: bfloat16 [2, 2048, 4096], P(None, ('scene', 'pulse')), parts along dimension 1
There are 2 independent parts, one for each index of `scene`. A program takes and returns all parts, laid end to end along the dimension named above; an argument that names none is the same for every part. Nothing has to cross between parts.
Inputs may be any that keep to these rules, and one draw needn't show every extreme that they name: half_table[l, s] + half_table[l, s XOR 2**l] == 1 for every level l and block s.
All inputs are finite; a program needn't handle non-finite values.
Results may differ from a plain program's by a relative error of at most 0.0074.
Values may be sent and summed in bfloat16 or wider, within the bound.
A program may use at most 64 MiB of HBM per device.

v0:
```python
import jax
import jax.numpy as jnp
from jax import lax
from jax.sharding import PartitionSpec as P

SHIFT = 48


def from_partner(value, axis, bit):
    mask = 2**bit
    pairs = [(source, source ^ mask) for source in range(lax.axis_size(axis))]
    return lax.ppermute(value, axis, pairs)


def band_matrix(ukern, half, count, utaps):
    width = count // 2 + utaps
    local = jnp.arange(count, dtype=jnp.int32)
    rows = half * count + local
    cols = half * (count // 2) + jnp.arange(width, dtype=jnp.int32)
    offset = cols[None, :] - rows[:, None] // 2 - 1
    kernel = jnp.where(
        (local % 2 == 0)[:, None],
        ukern[0].astype(jnp.float32)[None, :],
        ukern[1].astype(jnp.float32)[None, :],
    )
    picks = (offset[:, :, None] == jnp.arange(utaps, dtype=jnp.int32)[None, None, :]).astype(
        jnp.float32
    )
    return jnp.sum(picks * kernel[:, None, :], axis=2).astype(jnp.bfloat16)


def tap_weights(tap_row, rkern):
    onehot = (tap_row[:, None] == jnp.arange(rkern.shape[0], dtype=jnp.int32)[None, :]).astype(
        jnp.float32
    )
    return jnp.dot(
        onehot, rkern, precision=lax.Precision.HIGHEST, preferred_element_type=jnp.float32
    )


def child_term(range_band, sample_window, weights, shift, segment):
    blended_beam = jnp.einsum(
        "dp,upe->ude", range_band, sample_window, preferred_element_type=jnp.float32
    )
    length = blended_beam.shape[2]
    margin = SHIFT + weights.shape[1]
    padded = jnp.pad(blended_beam, ((0, 0), (0, 0), (margin, margin)))
    shifted = jnp.zeros(blended_beam.shape, jnp.float32)
    for tap in range(weights.shape[1]):
        piece = lax.dynamic_slice_in_dim(padded, margin + shift + tap - 1, length, 2)
        shifted = shifted + weights[None, :, tap, None] * piece
    cosine = jnp.cos(segment)[:, None]
    sine = jnp.sin(segment)[:, None]
    real_part = cosine * shifted[0] - sine * shifted[1]
    imag_part = sine * shifted[0] + cosine * shifted[1]
    return jnp.stack([real_part, imag_part])


def on_device(beams, ukern, rkern, angles, taps, shifts, half_table):
    count = beams.shape[1]
    utaps = ukern.shape[1]
    width = count // 2 + utaps
    myself = lax.axis_index("pulse")
    current = beams
    for level in range(half_table.shape[0]):
        partner = jnp.bitwise_xor(myself, 1 << level)
        half = half_table[level, myself]
        range_band = band_matrix(ukern, half, count, utaps)
        own_pad = jnp.pad(current, ((0, 0), (utaps // 2, utaps // 2), (0, 0)))
        own_window = lax.dynamic_slice_in_dim(own_pad, half * (count // 2), width, 1)
        outbound_rows = lax.dynamic_slice_in_dim(own_pad, (1 - half) * (count // 2), width, 1)
        far_window = from_partner(outbound_rows, "pulse", level)
        weights = tap_weights(taps[level], rkern)
        own_bit = jnp.bitwise_and(jnp.right_shift(myself, level), 1)
        own_row = jnp.where(own_bit == 0, angles[level, 0], angles[level, 1])
        distant_row = jnp.where(own_bit == 0, angles[level, 1], angles[level, 0])
        own_seg = lax.dynamic_slice_in_dim(own_row, half * count, count, 0)
        far_seg = lax.dynamic_slice_in_dim(distant_row, half * count, count, 0)
        own_term = child_term(range_band, own_window, weights, shifts[level, myself], own_seg)
        far_term = child_term(range_band, far_window, weights, shifts[level, partner], far_seg)
        current = (0.70710678 * (own_term + far_term)).astype(jnp.bfloat16)
    return current


def solution(mesh):
    in_specs = (
        P(None, ("scene", "pulse"), None),
        P(),
        P(),
        P(),
        P(None, ("scene", "pulse")),
        P(),
        P(),
    )
    out_specs = P(None, ("scene", "pulse"), None)
    return jax.shard_map(
        on_device, mesh=mesh, in_specs=in_specs, out_specs=out_specs, check_vma=False
    )
```

profile of v0, /device:TPU:0, one launch (start us, length us, event | category | flops | bytes accessed | tf_op | source)
XLA Modules:
  0.0 147.4 jit_solution(9022183245340307306)
XLA Ops:
  0.0 1.5 %constant_dynamic-slice_fusion.7 = (s32[1,1]{1,0:T(1,128)}, s32[1,1]{1,0:T(1,128)}, s32[1,1]{1,0:T(1,128)}, s32[1,1]{1,0:T(1,128)}) fusion(s32[4,16]{1,0:T(4,128)} %param.13, s32[]{:T(128)S(6)} %select_n.272), kind=kLoop, calls=%fused_computation.96 | loop fusion | bytes 36 | tf_op jit(solution)/shard_map/dynamic_slice | solution.py:67
  2.2 1.3 pad_dynamic-slice_fusion.6
  3.4 0.6 collective-permute-start
  8.9 0.7 constant_dynamic-slice_fusion.17
  20.7 0.1 subtract_add_fusion.2
  20.8 0.1 subtract_add_fusion.3
  20.9 1.3 select_reduce_fusion
  22.3 0.1 cosine_bitcast_fusion.3
  22.5 0.2 fusion.11
  22.7 0.4 convolution_bitcast_fusion.7
  23.2 0.4 convolution_bitcast_fusion.6
  23.6 4.5 %multiply_add_fusion.6 = (f32[2,64,4096]{2,1,0:T(8,128)S(1)}, f32[2,64,4096]{2,1,0:T(8,128)S(1)}) fusion(s32[]{:T(128)S(6)} %select_n.297, s32[]{:T(128)S(6)} %select_n.296, s32[]{:T(128)S(6)} %select_n.295, s32[]{:T(128)S(6)} %select_n.294, f32[2,64,4096]{2,1,0:T(8,128)S(1)} %convolution_bitcast_fusion.6, f32[64]{0:T(128)S(1)} %get-tuple-element.65, ...), kind=kLoop, calls=%fused_computation.26 | loop fusion | flops 7340032 | bytes 8389664 | tf_op jit(solution)/shard_map/add | solution.py:51
  28.1 0.3 multiply_subtract_fusion.6
  28.4 0.3 multiply_subtract_fusion.7
  28.8 0.3 fusion.1
  29.0 0.1 pad_dynamic-slice_fusion.4
  29.2 2.6 %collective-permute-start.1 = (bf16[2,64,4096]{2,1,0:T(8,128)(2,1)S(1)}, bf16[2,64,4096]{2,1,0:T(8,128)(2,1)S(1)}, u32[]{:S(2)}, u32[]{:S(2)}) collective-permute-start(bf16[2,64,4096]{2,1,0:T(8,128)(2,1)S(1)} %pad_dynamic-slice_fusion.4), channel_id=1, source_target_pairs={{0,2},{1,3},{2,0},{3,1},{4,6},{5,7},{6,4},{7,5},{8,10},{9,11},{10,... | collective-permute-start | bytes 3145736 | tf_op jit(solution)/shard_map/ppermute | solution.py:12
  42.3 0.1 cosine_bitcast_fusion.2
  42.4 0.2 fusion.10
  42.6 0.5 convolution_bitcast_fusion.5
  43.1 12.5 %collective-permute-done.1 = bf16[2,64,4096]{2,1,0:T(8,128)(2,1)S(1)} collective-permute-done((bf16[2,64,4096]{2,1,0:T(8,128)(2,1)S(1)}, bf16[2,64,4096]{2,1,0:T(8,128)(2,1)S(1)}, u32[]{:S(2)}, u32[]{:S(2)}) %collective-permute-start.1) | collective-permute-done | bytes 1048608 | tf_op jit(solution)/shard_map/ppermute | solution.py:12
  55.6 0.4 convolution_bitcast_fusion.4
  56.0 4.7 %multiply_add_fusion.4 = (f32[2,64,4096]{2,1,0:T(8,128)S(1)}, f32[2,64,4096]{2,1,0:T(8,128)S(1)}) fusion(s32[]{:T(128)S(6)} %select_n.310, s32[]{:T(128)S(6)} %select_n.309, s32[]{:T(128)S(6)} %select_n.308, s32[]{:T(128)S(6)} %select_n.307, f32[2,64,4096]{2,1,0:T(8,128)S(1)} %convolution_bitcast_fusion.4, f32[64]{0:T(128)S(1)} %get-tuple-element.59, ...), kind=kLoop, calls=%fused_computation.24 | loop fusion | flops 7340032 | bytes 8389664 | tf_op jit(solution)/shard_map/add | solution.py:51
  60.7 0.3 multiply_subtract_fusion.4
  61.0 0.3 multiply_subtract_fusion.5
  61.3 0.3 fusion.3
  61.6 0.1 pad_dynamic-slice_fusion.2
  61.8 2.1 %collective-permute-start.2 = (bf16[2,64,4096]{2,1,0:T(8,128)(2,1)S(1)}, bf16[2,64,4096]{2,1,0:T(8,128)(2,1)S(1)}, u32[]{:S(2)}, u32[]{:S(2)}) collective-permute-start(bf16[2,64,4096]{2,1,0:T(8,128)(2,1)S(1)} %pad_dynamic-slice_fusion.2), channel_id=1, source_target_pairs={{0,4},{1,5},{2,6},{3,7},{4,0},{5,1},{6,2},{7,3},{8,12},{9,13},{10,... | collective-permute-start | bytes 3145736 | tf_op jit(solution)/shard_map/ppermute | solution.py:12
  84.9 0.1 cosine_bitcast_fusion.1
  85.0 0.2 fusion.9
  85.2 0.5 convolution_bitcast_fusion.3
  85.7 1.2 collective-permute-done.2
  86.8 0.4 convolution_bitcast_fusion.2
  87.2 4.5 %multiply_add_fusion.2 = (f32[2,64,4096]{2,1,0:T(8,128)S(1)}, f32[2,64,4096]{2,1,0:T(8,128)S(1)}) fusion(s32[]{:T(128)S(6)} %select_n.323, s32[]{:T(128)S(6)} %select_n.322, s32[]{:T(128)S(6)} %select_n.321, s32[]{:T(128)S(6)} %select_n.320, f32[2,64,4096]{2,1,0:T(8,128)S(1)} %convolution_bitcast_fusion.2, f32[64]{0:T(128)S(1)} %get-tuple-element.53, ...), kind=kLoop, calls=%fused_computation.22 | loop fusion | flops 7340032 | bytes 8389664 | tf_op jit(solution)/shard_map/add | solution.py:51
  91.7 0.3 multiply_subtract_fusion.2
  92.1 0.3 multiply_subtract_fusion.3
  92.4 0.3 fusion.5
  92.7 0.1 pad_dynamic-slice_fusion
  92.8 2.6 %collective-permute-start.3 = (bf16[2,64,4096]{2,1,0:T(8,128)(2,1)S(1)}, bf16[2,64,4096]{2,1,0:T(8,128)(2,1)S(1)}, u32[]{:S(2)}, u32[]{:S(2)}) collective-permute-start(bf16[2,64,4096]{2,1,0:T(8,128)(2,1)S(1)} %pad_dynamic-slice_fusion), channel_id=1, source_target_pairs={{0,8},{1,9},{2,10},{3,11},{4,12},{5,13},{6,14},{7,15},{8,0},{9,1},... | collective-permute-start | bytes 3145736 | tf_op jit(solution)/shard_map/ppermute | solution.py:12
  95.4 0.1 cosine_bitcast_fusion
  95.5 0.2 fusion.8
  95.7 0.5 convolution_bitcast_fusion.1
  96.2 44.2 %collective-permute-done.3 = bf16[2,64,4096]{2,1,0:T(8,128)(2,1)S(1)} collective-permute-done((bf16[2,64,4096]{2,1,0:T(8,128)(2,1)S(1)}, bf16[2,64,4096]{2,1,0:T(8,128)(2,1)S(1)}, u32[]{:S(2)}, u32[]{:S(2)}) %collective-permute-start.3) | collective-permute-done | bytes 1048608 | tf_op jit(solution)/shard_map/ppermute | solution.py:12
  140.4 0.4 convolution_bitcast_fusion
  140.8 4.7 %multiply_add_fusion = (f32[2,64,4096]{2,1,0:T(8,128)S(1)}, f32[2,64,4096]{2,1,0:T(8,128)S(1)}) fusion(s32[]{:T(128)S(6)} %select_n.336, s32[]{:T(128)S(6)} %select_n.335, s32[]{:T(128)S(6)} %select_n.334, s32[]{:T(128)S(6)} %select_n.333, f32[2,64,4096]{2,1,0:T(8,128)S(1)} %convolution_bitcast_fusion, f32[64]{0:T(128)S(1)} %get-tuple-element.43, ...), kind=kLoop, calls=%fused_computation.20 | loop fusion | flops 7340032 | bytes 8389664 | tf_op jit(solution)/shard_map/add | solution.py:51
  145.5 0.3 multiply_subtract_fusion
  145.8 0.3 multiply_subtract_fusion.1
  146.2 1.2 fusion.7
  (31 shorter events, 0.4 us)
Async XLA Ops:
  0.0 22.5 %copy-start = (f32[16,4]{0,1:T(4,128)S(1)}, f32[16,4]{0,1:T(4,128)}, u32[]{:S(2)}) copy-start(f32[16,4]{0,1:T(4,128)} %param.9) | copy-start | bytes 772
  0.0 22.7 %copy-start.1 = (bf16[2,64,4096]{2,1,0:T(8,128)(2,1)S(1)}, bf16[2,64,4096]{2,1,0:T(8,128)(2,1)}, u32[]{:S(2)}) copy-start(bf16[2,64,4096]{2,1,0:T(8,128)(2,1)} %param.7) | copy-start | bytes 3145732
  0.0 8.9 %copy-start.2 = (s32[4,16]{1,0:T(4,128)S(1)}, s32[4,16]{1,0:T(4,128)}, u32[]{:S(2)}) copy-start(s32[4,16]{1,0:T(4,128)} %param.12) | copy-start | bytes 772
  0.0 20.4 %copy-start.5 = (bf16[2,32]{1,0:T(2,128)(2,1)S(1)}, bf16[2,32]{1,0:T(2,128)(2,1)}, u32[]{:S(2)}) copy-start(bf16[2,32]{1,0:T(2,128)(2,1)} %param.8) | copy-start | bytes 388
  0.0 22.3 %copy-start.3 = (f32[4,2,128]{2,1,0:T(2,128)S(1)}, f32[4,2,128]{2,1,0:T(2,128)}, u32[]{:S(2)}) copy-start(f32[4,2,128]{2,1,0:T(2,128)} %param.10) | copy-start | bytes 12292
  0.0 22.4 %copy-start.4 = (s32[4,64]{1,0:T(4,128)S(1)}, s32[4,64]{1,0:T(4,128)}, u32[]{:S(2)}) copy-start(s32[4,64]{1,0:T(4,128)} %param.11) | copy-start | bytes 3076
  3.4 19.7 %collective-permute-start = (bf16[2,64,4096]{2,1,0:T(8,128)(2,1)S(1)}, bf16[2,64,4096]{2,1,0:T(8,128)(2,1)S(1)}, u32[]{:S(2)}, u32[]{:S(2)}) collective-permute-start(bf16[2,64,4096]{2,1,0:T(8,128)(2,1)S(1)} %pad_dynamic-slice_fusion.6), channel_id=1, source_target_pairs={{0,1},{1,0},{2,3},{3,2},{4,5},{5,4},{6,7},{7,6},{8,9},{9,8},{10,11... | collective-permute-start | bytes 3145736 | tf_op jit(solution)/shard_map/ppermute | solution.py:12
  29.2 26.4 %collective-permute-start.1 = (bf16[2,64,4096]{2,1,0:T(8,128)(2,1)S(1)}, bf16[2,64,4096]{2,1,0:T(8,128)(2,1)S(1)}, u32[]{:S(2)}, u32[]{:S(2)}) collective-permute-start(bf16[2,64,4096]{2,1,0:T(8,128)(2,1)S(1)} %pad_dynamic-slice_fusion.4), channel_id=1, source_target_pairs={{0,2},{1,3},{2,0},{3,1},{4,6},{5,7},{6,4},{7,5},{8,10},{9,11},{10,... | collective-permute-start | bytes 3145736 | tf_op jit(solution)/shard_map/ppermute | solution.py:12
  61.8 25.1 %collective-permute-start.2 = (bf16[2,64,4096]{2,1,0:T(8,128)(2,1)S(1)}, bf16[2,64,4096]{2,1,0:T(8,128)(2,1)S(1)}, u32[]{:S(2)}, u32[]{:S(2)}) collective-permute-start(bf16[2,64,4096]{2,1,0:T(8,128)(2,1)S(1)} %pad_dynamic-slice_fusion.2), channel_id=1, source_target_pairs={{0,4},{1,5},{2,6},{3,7},{4,0},{5,1},{6,2},{7,3},{8,12},{9,13},{10,... | collective-permute-start | bytes 3145736 | tf_op jit(solution)/shard_map/ppermute | solution.py:12
  92.8 47.6 %collective-permute-start.3 = (bf16[2,64,4096]{2,1,0:T(8,128)(2,1)S(1)}, bf16[2,64,4096]{2,1,0:T(8,128)(2,1)S(1)}, u32[]{:S(2)}, u32[]{:S(2)}) collective-permute-start(bf16[2,64,4096]{2,1,0:T(8,128)(2,1)S(1)} %pad_dynamic-slice_fusion), channel_id=1, source_target_pairs={{0,8},{1,9},{2,10},{3,11},{4,12},{5,13},{6,14},{7,15},{8,0},{9,1},... | collective-permute-start | bytes 3145736 | tf_op jit(solution)/shard_map/ppermute | solution.py:12
where the time goes:
time: 148 us; the launch traced here: 147 us
  waiting for transfers between devices  57.9 us (39%)
  between operations  48.4 us (33%)
  other arithmetic  24.7 us (17%)
  starting transfers between devices  7.75 us (5%)
  local copies, waits for them, and re-layouts  4.43 us (3%)
  matrix products  4.23 us (3%)
    ppermute x4, waiting for transfers between devices, from_partner(): return lax.ppermute(value, axis, pairs)  57.9 us
    add x4, other arithmetic, child_term(): shifted = shifted + weights[None, :, tap, None] * piece  18.3 us
    ppermute x4, starting transfers between devices, from_partner(): return lax.ppermute(value, axis, pairs)  7.75 us
    dot_general x8, matrix products, child_term(): jnp.einsum('dp,upe->ude', range_band, sample_window, preferred_element_ty...  3.5 us
  transfers between devices with their start and end apart: 4, of which 3 were waited for; matrix products, arithmetic and copies ran while one was open for 4% of the time, Pallas kernels for 0%

commit v1 on v0

v1 whole, which is shorter than its diff:
```python
import functools

import jax
import jax.numpy as jnp
from jax import lax
from jax.experimental import pallas as pl
from jax.experimental.pallas import tpu as pltpu
from jax.sharding import PartitionSpec as P

MESH = pl.DeviceIdType.MESH
LANES = 128
CHUNK = 256
GAP = 2


def tables(ukern, rkern, angles, taps, half_table, count):
    levels, utaps = half_table.shape[0], ukern.shape[1]
    window = (count + utaps) // 2
    me = lax.axis_index("pulse")
    half = half_table[:, me]
    own_bit = jnp.right_shift(me, jnp.arange(levels, dtype=jnp.int32)) & 1
    by_child = jnp.where((own_bit == 0)[:, None, None], angles, angles[:, ::-1])
    segment = jnp.where(
        (half == 0)[:, None, None], by_child[:, :, :count], by_child[:, :, count:]
    )
    cosine = 0.70710678 * jnp.cos(segment)
    sine = 0.70710678 * jnp.sin(segment)
    turn = jnp.stack([jnp.stack([cosine, -sine], 2), jnp.stack([sine, cosine], 2)], 2)
    phases = jnp.arange(rkern.shape[0], dtype=jnp.int32)
    weights = jnp.sum(
        jnp.where((taps[:, :, None] == phases)[..., None], rkern[None, None], 0.0), axis=2
    )
    beam = jnp.arange(count, dtype=jnp.int32)
    kernel = jnp.where(
        (beam % 2 == 0)[:, None], ukern[0].astype(jnp.float32), ukern[1].astype(jnp.float32)
    )

    def one(child, rows, step):
        first = utaps // 2 - 1 - step * half
        offset = (
            first[:, None, None]
            + jnp.arange(rows, dtype=jnp.int32)[None, None, :]
            - (beam // 2)[None, :, None]
        )
        band = jnp.sum(
            jnp.where(
                offset[..., None] == jnp.arange(utaps, dtype=jnp.int32),
                kernel[None, :, None, :],
                0.0,
            ),
            axis=3,
        )
        matrix = (
            turn[:, child].transpose(0, 1, 3, 2)[:, :, :, None, :, None]
            * weights[:, None, :, :, None, None]
            * band[:, None, :, None, None, :]
        )
        return matrix.reshape(levels, 2 * count, -1).astype(jnp.bfloat16)

    return one(0, count, count // 2), one(1, window, utaps // 2)


def shifted_taps(left, mid, right, shift, ntaps):
    width = mid.shape[1]
    full = jnp.concatenate([left, mid, right], axis=1).astype(jnp.float32)
    total = full.shape[1]
    out = []
    for tap in range(ntaps):
        amount = lax.rem(2 * total - (shift + tap - 1), total)
        moved = pltpu.roll(full, amount, 1)
        out.append(moved[:, LANES : LANES + width].astype(jnp.bfloat16))
    return jnp.concatenate(out, axis=0)


def merge_kernel(
    window, ntaps, shifts_ref, half_ref, x_ref, own_ref, far_ref, out_ref,
    block, outbox, inbox, send_sem, recv_sem,
):
    levels, count = own_ref.shape[0], own_ref.shape[1] // 2
    chunks = inbox.shape[1] - 2
    me = lax.axis_index("pulse")
    partners = []
    for level in range(levels):
        bit = lax.rem(me // 2**level, 2)
        partners.append(me + (1 - 2 * bit) * 2**level)

    barrier = pltpu.get_barrier_semaphore()
    for partner in partners:
        pl.semaphore_signal(barrier, inc=1, device_id={"pulse": partner}, device_id_type=MESH)
    pl.semaphore_wait(barrier, levels)

    for level in range(levels):
        for edge in (0, chunks + 1):
            block[level, edge] = jnp.zeros_like(block[level, edge])
            inbox[level, edge] = jnp.zeros_like(inbox[level, edge])

    def copy(level, chunk):
        return pltpu.make_async_remote_copy(
            src_ref=outbox.at[level, chunk],
            dst_ref=inbox.at[level, chunk + 1],
            send_sem=send_sem.at[level, chunk],
            recv_sem=recv_sem.at[level, chunk],
            device_id={"pulse": partners[level]},
            device_id_type=MESH,
        )

    def hand_over(level, chunk, value):
        block[level, chunk + 1] = value
        high = half_ref[level, me] == 0
        parts = []
        for part in range(2):
            rows = value[part * count : (part + 1) * count]
            parts.append(jnp.where(high, rows[count - window :], rows[:window]))
        outbox[level, chunk] = jnp.concatenate(parts, axis=0)
        copy(level, chunk).start()

    def pieces(ref, level, chunk):
        return (
            ref[level, chunk, :, CHUNK - LANES :],
            ref[level, chunk + 1],
            ref[level, chunk + 2, :, :LANES],
        )

    def work(level, chunk):
        partner = partners[level]
        near = shifted_taps(*pieces(block, level, chunk), shifts_ref[level, me], ntaps)
        far = shifted_taps(*pieces(inbox, level, chunk), shifts_ref[level, partner], ntaps)
        total = jnp.dot(own_ref[level], near, preferred_element_type=jnp.float32)
        total = total + jnp.dot(far_ref[level], far, preferred_element_type=jnp.float32)
        value = total.astype(jnp.bfloat16)
        if level + 1 < levels:
            hand_over(level + 1, chunk, value)
        else:
            out_ref[:, pl.ds(pl.multiple_of(chunk * CHUNK, CHUNK), CHUNK)] = value

    @pl.loop(0, chunks)
    def _(chunk):
        columns = pl.ds(pl.multiple_of(chunk * CHUNK, CHUNK), CHUNK)
        hand_over(0, chunk, x_ref[:, columns])

    last_start = (levels - 1) * GAP

    @pl.loop(0, chunks + 1 + last_start)
    def _(step):
        for level in range(levels):
            coming = step - level * GAP

            @pl.when((coming >= 0) & (coming < chunks))
            def _():
                copy(level, coming).wait_recv()

            @pl.when((coming >= 1) & (coming <= chunks))
            def _():
                work(level, coming - 1)

    for level in range(levels):

        @pl.loop(0, chunks)
        def _(chunk):
            copy(level, chunk).wait_send()


def on_device(beams, ukern, rkern, angles, taps, shifts, half_table):
    parts, count, bins = beams.shape
    levels, utaps, ntaps = half_table.shape[0], ukern.shape[1], rkern.shape[1]
    window = (count + utaps) // 2
    chunks = bins // CHUNK
    own, far = tables(ukern, rkern, angles, taps, half_table, count)
    vmem = pl.BlockSpec(memory_space=pltpu.VMEM)
    smem = pl.BlockSpec(memory_space=pltpu.SMEM)
    merged = pl.pallas_call(
        functools.partial(merge_kernel, window, ntaps),
        out_shape=jax.ShapeDtypeStruct((parts * count, bins), jnp.bfloat16),
        in_specs=[smem, smem, vmem, vmem, vmem],
        out_specs=vmem,
        scratch_shapes=[
            pltpu.VMEM((levels, chunks + 2, parts * count, CHUNK), jnp.bfloat16),
            pltpu.VMEM((levels, chunks, parts * window, CHUNK), jnp.bfloat16),
            pltpu.VMEM((levels, chunks + 2, parts * window, CHUNK), jnp.bfloat16),
            pltpu.SemaphoreType.DMA((levels, chunks)),
            pltpu.SemaphoreType.DMA((levels, chunks)),
        ],
        compiler_params=pltpu.CompilerParams(collective_id=0, has_side_effects=True),
    )(shifts, half_table, beams.reshape(parts * count, bins), own, far)
    return merged.reshape(parts, count, bins)


def solution(mesh):
    in_specs = (
        P(None, ("scene", "pulse"), None),
        P(),
        P(),
        P(),
        P(None, ("scene", "pulse")),
        P(),
        P(),
    )
    out_specs = P(None, ("scene", "pulse"), None)
    return jax.shard_map(
        on_device, mesh=mesh, in_specs=in_specs, out_specs=out_specs, check_vma=False
    )
```

time: 148 us -> 90.8 us (0.61)
  Pallas kernels: 0 us -> 74.6 us
  waiting for transfers between devices: 57.9 us -> 0 us
  between operations: 48.4 us -> 0.16 us
  other arithmetic: 24.7 us -> 9.54 us
  starting transfers between devices: 7.75 us -> 0 us
  matrix products: 4.23 us -> 0 us
  local copies, waits for them, and re-layouts: 4.43 us -> 6.22 us
    pallas_call x0 -> x1, Pallas kernels: none -> 74.6 us  [on_device(): pl.pallas_call(functools.partial(merge_kernel, window, ntaps), out_shape=...]
    ppermute x4 -> x0, waiting for transfers between devices: 57.9 us -> none  [from_partner(): return lax.ppermute(value, axis, pairs)]
    add x8 -> x2, other arithmetic: 18.3 us -> 0.14 us  [one(): first[:, None, None] + jnp.arange(rows, dtype=jnp.int32)[None, None, :]]
    ppermute x4 -> x0, starting transfers between devices: 7.75 us -> none  [from_partner(): return lax.ppermute(value, axis, pairs)]
    dot_general x12 -> x0, matrix products: 4.23 us -> none  [the longest x8 3.5 us: child_term(): jnp.einsum('dp,upe->ude', range_band, sample_window, preferred_element_ty...]
    dynamic_slice x6 -> x0, local copies, waits for them, and re-layouts: 3.88 us -> none  [the longest x4 1.7 us: on_device(): lax.dynamic_slice_in_dim(own_pad, (1 - half) * (count // 2), width, 1)]
    convert_element_type x0 -> x3, local copies, waits for them, and re-layouts: none -> 2.68 us  [one(): return matrix.reshape(levels, 2 * count, -1).astype(jnp.bfloat16)]
    sub x12 -> x3, other arithmetic: 3 us -> 0.36 us  [the longest x1 0.19 us: one(): first = utaps // 2 - 1 - step * half]
  transfers between devices with their start and end apart: 4 -> 0, of which waited for: 3 -> 0; matrix products, arithmetic and copies ran while one was open for 4% -> 0% of each run, Pallas kernels for 0% -> 0%
where the time goes in v1:
time: 90.8 us; the launch traced here: 90.5 us
  Pallas kernels  74.6 us (82%)
  other arithmetic  9.54 us (11%)
  local copies, waits for them, and re-layouts  6.22 us (7%)
    pallas_call x1, Pallas kernels, on_device(): pl.pallas_call(functools.partial(merge_kernel, window, ntaps), out_shape=...  74.6 us
    convert_element_type x2, other arithmetic, one(): return matrix.reshape(levels, 2 * count, -1).astype(jnp.bfloat16)  3.2 us
    convert_element_type x3, local copies, waits for them, and re-layouts, one(): return matrix.reshape(levels, 2 * count, -1).astype(jnp.bfloat16)  2.68 us
    reduce_sum x2, other arithmetic, one(): jnp.sum(jnp.where(offset[..., None] == jnp.arange(utaps, dtype=jnp.int32)...  2.3 us
    unnamed x5, local copies, waits for them, and re-layouts  2.3 us

profile of v1, /device:TPU:0, one launch (start us, length us, event | category | flops | bytes accessed | tf_op | source)
XLA Modules:
  0.0 90.5 jit_solution(12930150967876847189)
XLA Ops:
  0.0 0.0 copy-start
  0.0 0.0 copy-start.1
  0.0 0.9 %compare_reduce_fusion = pred[4]{0:T(512)(128)(4,1)S(1)} fusion(s32[4,16]{1,0:T(4,128)} %half_ref.1, s32[]{:T(128)S(6)} %select_n.54), kind=kLoop, calls=%fused_computation.31 | loop fusion | flops 4 | bytes 24 | tf_op jit(solution)/shard_map/eq | solution.py:24
  0.9 0.7 rev.3
  1.7 0.8 broadcast_select_fusion.1
  2.4 0.1 fusion.1
  2.6 0.1 multiply_bitcast_fusion
  2.7 0.7 iota_compare_fusion.2
  3.4 0.8 select_reduce_fusion.2
  4.2 0.5 copy.17
  4.7 0.0 copy-done
  4.7 0.2 subtract_reduce_fusion
  4.9 0.1 iota_add_fusion.1
  5.0 0.1 broadcast_subtract_fusion
  5.1 0.0 copy-done.1
  5.1 0.1 broadcast_select_fusion
  5.2 1.3 %select_reduce_fusion = f32[4,64,64]{2,1,0:T(8,128)S(1)} fusion(f32[64,32]{1,0:T(8,128)S(1)} %broadcast_select_fusion, s32[4,64,64]{2,1,0:T(8,128)S(1)} %broadcast_subtract_fusion), kind=kLoop, calls=%fused_computation | loop fusion | flops 1556480 | bytes 139264 | tf_op jit(solution)/shard_map/reduce_sum | solution.py:45
  6.5 2.5 %multiply_convert_fusion = bf16[4,2,64,4,2,64]{5,4,3,2,1,0:T(2,128)(2,1)S(1)} fusion(f32[4,64,64]{2,1,0:T(8,128)S(1)} %select_reduce_fusion, f32[4,2,64,4,2]{4,3,2,1,0:T(4,128)S(1)} %copy.17), kind=kLoop, calls=%fused_computation.4 | loop fusion | flops 524288 | bytes 606208 | tf_op jit(solution)/shard_map/convert_element_type | solution.py:58
  8.9 1.4 %convert_element_type.27.own_ref = bf16[4,128,512]{2,1,0:T(8,128)(2,1)} reshape(bf16[4,2,64,4,2,64]{5,4,3,2,1,0:T(2,128)(2,1)S(1)} %multiply_convert_fusion) | data formatting | bytes 1048576 | tf_op jit(solution)/shard_map/convert_element_type | solution.py:58
  10.4 0.1 iota_add_fusion
  10.4 0.1 broadcast_subtract_fusion.1
  10.5 0.1 copy.19
  10.6 1.0 %select_reduce_fusion.1 = f32[4,64,48]{1,2,0:T(8,128)S(1)} fusion(f32[64,32]{0,1:T(8,128)S(1)} %copy.19, s32[4,64,48]{1,2,0:T(8,128)S(1)} %broadcast_subtract_fusion.1), kind=kLoop, calls=%fused_computation.2 | loop fusion | flops 1167360 | bytes 106496 | tf_op jit(solution)/shard_map/reduce_sum | solution.py:45
  11.6 0.7 multiply_convert_fusion.1
  12.3 0.3 convert_element_type.29
  12.7 0.9 %copy.20.far_ref = bf16[4,128,384]{2,1,0:T(8,128)(2,1)} copy(bf16[4,128,384]{1,2,0:T(8,128)(2,1)S(1)} %convert_element_type.29) | data formatting | bytes 786432 | tf_op jit(solution)/shard_map/convert_element_type | solution.py:58
  13.6 74.6 %shard_map.73 = bf16[128,4096]{1,0:T(8,128)(2,1)} custom-call(s32[4,16]{1,0:T(4,128)} %shifts_ref.1, s32[4,16]{1,0:T(4,128)} %half_ref.1, bf16[128,4096]{1,0:T(8,128)(2,1)} %bitcast.27, bf16[4,128,512]{2,1,0:T(8,128)(2,1)} %convert_element_type.27.own_ref, bf16[4,128,384]{2,1,0:T(8,128)(2,1)} %copy.20.far_ref), custom_call_target="tpu_custom_call" | custom-call | tf_op jit(solution)/shard_map/pallas_call | solution.py:171
  88.2 2.3 %copy.22 = bf16[2,64,4096]{2,1,0:T(8,128)(2,1)} copy(bf16[2,64,4096]{2,1,0:T(8,128)(2,1)} %bitcast.26) | data formatting | bytes 2097152
  (9 shorter events, 0.1 us)
Async XLA Ops:
  0.0 4.7 %copy-start = (s32[4,16]{1,0:T(4,128)S(1)}, s32[4,16]{1,0:T(4,128)}, u32[]{:S(2)}) copy-start(s32[4,16]{1,0:T(4,128)} %half_ref.1) | copy-start | bytes 772
  0.0 5.1 %copy-start.1 = (bf16[2,32]{1,0:T(2,128)(2,1)S(1)}, bf16[2,32]{1,0:T(2,128)(2,1)}, u32[]{:S(2)}) copy-start(bf16[2,32]{1,0:T(2,128)(2,1)} %param.8) | copy-start | bytes 388

commit v2 on v1

v2 whole, which is shorter than its diff:
```python
import functools

import jax
import jax.numpy as jnp
from jax import lax
from jax.experimental import pallas as pl
from jax.experimental.pallas import tpu as pltpu
from jax.sharding import PartitionSpec as P

MESH = pl.DeviceIdType.MESH
LANES = 128
CHUNK = 256
ROLLED = jnp.bfloat16
GAP = 2


def band_base(ukern_ref, count):
    utaps = ukern_ref.shape[1]
    beam = lax.broadcasted_iota(jnp.int32, (count, LANES), 0)
    tap = lax.broadcasted_iota(jnp.int32, (count, LANES), 1) - lax.div(beam, 2) - 1
    even = lax.rem(beam, 2) == 0
    base = jnp.zeros((count, LANES), jnp.float32)
    for k in range(utaps):
        base = jnp.where(tap == k, jnp.where(even, ukern_ref[0, k], ukern_ref[1, k]), base)
    return base


def band(base, first, rows):
    lane = lax.broadcasted_iota(jnp.int32, base.shape, 1)
    low = pltpu.roll(base, lax.rem(2 * LANES - first, LANES), 1)
    high = pltpu.roll(base, lax.rem(2 * LANES - first + rows, LANES), 1)
    return jnp.where(lane < rows, low, high)


def level_matrix(base, first, rows, segment, weights):
    cosine = 0.70710678 * jnp.cos(segment)
    sine = 0.70710678 * jnp.sin(segment)
    turns = (jnp.concatenate([cosine, sine], 1), jnp.concatenate([-sine, cosine], 1))
    lines = [jnp.concatenate([w, w], 1) * turn for w in weights for turn in turns]
    columns = jnp.transpose(jnp.concatenate(lines, axis=0))
    one = band(base, first, rows)
    both = jnp.concatenate([one, one], axis=0)
    lane = lax.broadcasted_iota(jnp.int32, both.shape, 1)
    out = []
    for tap in range(len(weights)):
        scale = jnp.where(
            lane < rows, columns[:, 2 * tap : 2 * tap + 1], columns[:, 2 * tap + 1 : 2 * tap + 2]
        )
        out.append((scale * both)[:, : 2 * rows])
    return jnp.concatenate(out, axis=1)


def shifted_taps(tiles, shift, ntaps):
    lane = lax.broadcasted_iota(jnp.int32, tiles[0].shape, 1)
    out = []
    for tap in range(ntaps):
        move = shift + (tap - 1)
        back = move < 0
        place = lax.rem(move + LANES, LANES)
        turned = [
            pltpu.roll(jnp.where(back, low, high), lax.rem(LANES - place, LANES), 1)
            for low, high in zip(tiles[:-1], tiles[1:])
        ]
        keep = lane < LANES - place
        moved = [jnp.where(keep, low, high) for low, high in zip(turned[:-1], turned[1:])]
        out.append(jnp.concatenate(moved, axis=1).astype(jnp.bfloat16))
    return jnp.concatenate(out, axis=0)


def merge_kernel(
    window, shifts_ref, half_ref, rkern_ref, ukern_ref, angles_ref, taps_ref, x_ref, out_ref,
    block, outbox, inbox, own_ref, far_ref, send_sem, recv_sem,
):
    levels, count = own_ref.shape[0], own_ref.shape[1] // 2
    phases, ntaps = rkern_ref.shape
    chunks = inbox.shape[1] - 2
    me = lax.axis_index("pulse")
    partners = []
    for level in range(levels):
        bit = lax.rem(me // 2**level, 2)
        partners.append(me + (1 - 2 * bit) * 2**level)

    barrier = pltpu.get_barrier_semaphore()
    for partner in partners:
        pl.semaphore_signal(barrier, inc=1, device_id={"pulse": partner}, device_id_type=MESH)
    pl.semaphore_wait(barrier, levels)

    for level in range(levels):
        for edge in (0, chunks + 1):
            block[level, edge] = jnp.zeros_like(block[level, edge])
            inbox[level, edge] = jnp.zeros_like(inbox[level, edge])

    def copy(level, chunk):
        return pltpu.make_async_remote_copy(
            src_ref=outbox.at[level, chunk],
            dst_ref=inbox.at[level, chunk + 1],
            send_sem=send_sem.at[level, chunk],
            recv_sem=recv_sem.at[level, chunk],
            device_id={"pulse": partners[level]},
            device_id_type=MESH,
        )

    def hand_over(level, chunk, value):
        block[level, chunk + 1] = value
        high = half_ref[level, me] == 0
        parts = []
        for part in range(2):
            rows = value[part * count : (part + 1) * count]
            parts.append(jnp.where(high, rows[count - window :], rows[:window]))
        outbox[level, chunk] = jnp.concatenate(parts, axis=0)
        copy(level, chunk).start()

    def pieces(ref, level, chunk):
        parts = [ref[level, chunk, :, CHUNK - LANES :]]
        for start in range(0, CHUNK, LANES):
            parts.append(ref[level, chunk + 1, :, start : start + LANES])
        parts.append(ref[level, chunk + 2, :, :LANES])
        return [part.astype(ROLLED) for part in parts]

    def work(level, chunk):
        partner = partners[level]
        near = shifted_taps(pieces(block, level, chunk), shifts_ref[level, me], ntaps)
        far = shifted_taps(pieces(inbox, level, chunk), shifts_ref[level, partner], ntaps)
        total = jnp.dot(own_ref[level], near, preferred_element_type=jnp.float32)
        total = total + jnp.dot(far_ref[level], far, preferred_element_type=jnp.float32)
        value = total.astype(jnp.bfloat16)
        if level + 1 < levels:
            hand_over(level + 1, chunk, value)
        else:
            out_ref[:, pl.ds(pl.multiple_of(chunk * CHUNK, CHUNK), CHUNK)] = value

    @pl.loop(0, chunks)
    def _(chunk):
        columns = pl.ds(pl.multiple_of(chunk * CHUNK, CHUNK), CHUNK)
        hand_over(0, chunk, x_ref[:, columns])

    base = band_base(ukern_ref, count)
    for level in range(levels):
        high = half_ref[level, me]
        segments = jnp.where(high == 0, angles_ref[level, :, :count], angles_ref[level, :, count:])
        upper = lax.rem(me // 2**level, 2) == 1
        here = jnp.where(upper, segments[1:2], segments[0:1])
        there = jnp.where(upper, segments[0:1], segments[1:2])
        phase = taps_ref[level : level + 1]
        weights = [jnp.zeros(phase.shape, jnp.float32)] * ntaps
        for number in range(phases):
            hit = phase == number
            weights = [jnp.where(hit, rkern_ref[number, t], w) for t, w in enumerate(weights)]
        pad = window - count // 2
        first = pad - high * (count // 2)
        own = level_matrix(base, first, count, here, weights)
        own_ref[level] = own.astype(jnp.bfloat16)
        far = level_matrix(base, first + high * (count - window), window, there, weights)
        far_ref[level] = far.astype(jnp.bfloat16)

    last_start = (levels - 1) * GAP

    @pl.loop(0, chunks + 1 + last_start)
    def _(step):
        for level in range(levels):
            coming = step - level * GAP

            @pl.when((coming >= 0) & (coming < chunks))
            def _():
                copy(level, coming).wait_recv()

            @pl.when((coming >= 1) & (coming <= chunks))
            def _():
                work(level, coming - 1)

    for level in range(levels):

        @pl.loop(0, chunks)
        def _(chunk):
            copy(level, chunk).wait_send()


def on_device(beams, ukern, rkern, angles, taps, shifts, half_table):
    parts, count, bins = beams.shape
    levels, utaps, ntaps = half_table.shape[0], ukern.shape[1], rkern.shape[1]
    window = (count + utaps) // 2
    chunks = bins // CHUNK
    vmem = pl.BlockSpec(memory_space=pltpu.VMEM)
    smem = pl.BlockSpec(memory_space=pltpu.SMEM)
    merged = pl.pallas_call(
        functools.partial(merge_kernel, window),
        out_shape=jax.ShapeDtypeStruct((parts * count, bins), jnp.bfloat16),
        in_specs=[smem, smem, smem, smem, vmem, vmem, vmem],
        out_specs=vmem,
        scratch_shapes=[
            pltpu.VMEM((levels, chunks + 2, parts * count, CHUNK), jnp.bfloat16),
            pltpu.VMEM((levels, chunks, parts * window, CHUNK), jnp.bfloat16),
            pltpu.VMEM((levels, chunks + 2, parts * window, CHUNK), jnp.bfloat16),
            pltpu.VMEM((levels, parts * count, ntaps * parts * count), jnp.bfloat16),
            pltpu.VMEM((levels, parts * count, ntaps * parts * window), jnp.bfloat16),
            pltpu.SemaphoreType.DMA((levels, chunks)),
            pltpu.SemaphoreType.DMA((levels, chunks)),
        ],
        compiler_params=pltpu.CompilerParams(collective_id=0, has_side_effects=True),
    )(
        shifts,
        half_table,
        rkern,
        ukern.astype(jnp.float32),
        angles,
        taps,
        beams.reshape(parts * count, bins),
    )
    return merged.reshape(parts, count, bins)


def solution(mesh):
    in_specs = (
        P(None, ("scene", "pulse"), None),
        P(),
        P(),
        P(),
        P(None, ("scene", "pulse")),
        P(),
        P(),
    )
    out_specs = P(None, ("scene", "pulse"), None)
    return jax.shard_map(
        on_device, mesh=mesh, in_specs=in_specs, out_specs=out_specs, check_vma=False
    )
```

time: 90.8 us -> 78.3 us (0.86)
  other arithmetic: 9.54 us -> 1.26 us
  local copies, waits for them, and re-layouts: 6.22 us -> 2.97 us
    reduce_sum x3 -> x0, other arithmetic: 3.08 us -> none  [the longest x2 2.3 us: one(): jnp.sum(jnp.where(offset[..., None] == jnp.arange(utaps, dtype=jnp.int32)...]
    convert_element_type x3 -> x0, local copies, waits for them, and re-layouts: 2.68 us -> none  [one(): return matrix.reshape(levels, 2 * count, -1).astype(jnp.bfloat16)]
    convert_element_type x3 -> x1, other arithmetic: 3.2 us -> 1.26 us  [on_device(): ukern.astype(jnp.float32)]
    eq x4 -> x0, other arithmetic: 1.64 us -> none  [the longest x1 0.94 us: tables(): half == 0]
    unnamed x5 -> x4, local copies, waits for them, and re-layouts: 2.3 us -> 2.97 us
where the time goes in v2:
time: 78.3 us; the launch traced here: 78.1 us
  Pallas kernels  73.9 us (94%)
  local copies, waits for them, and re-layouts  2.97 us (4%)
  other arithmetic  1.26 us (2%)
    pallas_call x1, Pallas kernels, on_device(): pl.pallas_call(functools.partial(merge_kernel, window), out_shape=jax.Sha...  73.9 us
    unnamed x4, local copies, waits for them, and re-layouts  2.97 us

profile of v2, /device:TPU:0, one launch (start us, length us, event | category | flops | bytes accessed | tf_op | source)
XLA Modules:
  0.0 78.1 jit_solution(9762933709630187370)
XLA Ops:
  0.0 0.0 copy-start
  0.0 1.3 %convert_element_type.3.ukern_ref = f32[2,32]{1,0:T(2,128)} convert(bf16[2,32]{1,0:T(2,128)(2,1)} %param.8) | non-fusion elementwise | flops 64 | bytes 384 | tf_op jit(solution)/shard_map/convert_element_type | solution.py:204
  1.3 0.0 copy-done
  1.3 0.7 copy.8.rkern_ref
  1.9 73.9 %shard_map.73 = bf16[128,4096]{1,0:T(8,128)(2,1)} custom-call(s32[4,16]{1,0:T(4,128)} %shifts_ref.1, s32[4,16]{1,0:T(4,128)} %half_ref.1, f32[16,4]{1,0:T(8,128)} %copy.8.rkern_ref, f32[2,32]{1,0:T(2,128)} %convert_element_type.3.ukern_ref, f32[4,2,128]{2,1,0:T(2,128)} %angles_ref.1, s32[4,64]{1,0:T(4,128)} %taps_ref.1, bf16[128,4096]{1,0:T(8,128)(2,1)} %bitcast.3), custom_call_target="tpu_custom_call" | custom-call | tf_op jit(solution)/shard_map/pallas_call | solution.py:185
  75.8 2.3 %copy.10 = bf16[2,64,4096]{2,1,0:T(8,128)(2,1)} copy(bf16[2,64,4096]{2,1,0:T(8,128)(2,1)} %bitcast.2) | data formatting | bytes 2097152
Async XLA Ops:
  0.0 1.3 %copy-start = (f32[16,4]{0,1:T(4,128)S(1)}, f32[16,4]{0,1:T(4,128)}, u32[]{:S(2)}) copy-start(f32[16,4]{0,1:T(4,128)} %param.9) | copy-start | bytes 772

commit v3 on v2

--- a/solution.py
+++ b/solution.py
@@ -11,17 +11,19 @@
 LANES = 128
 CHUNK = 256
 ROLLED = jnp.bfloat16
-GAP = 2
-
-
-def band_base(ukern_ref, count):
-    utaps = ukern_ref.shape[1]
+GAP = 3
+LAST = 4
+
+
+def band_base(ukern, count):
+    utaps = ukern.shape[1]
     beam = lax.broadcasted_iota(jnp.int32, (count, LANES), 0)
     tap = lax.broadcasted_iota(jnp.int32, (count, LANES), 1) - lax.div(beam, 2) - 1
     even = lax.rem(beam, 2) == 0
     base = jnp.zeros((count, LANES), jnp.float32)
     for k in range(utaps):
-        base = jnp.where(tap == k, jnp.where(even, ukern_ref[0, k], ukern_ref[1, k]), base)
+        column = ukern[:, k : k + 1]
+        base = jnp.where(tap == k, jnp.where(even, column[0:1], column[1:2]), base)
     return base
 
 
@@ -50,6 +52,12 @@
     return jnp.concatenate(out, axis=1)
 
 
+def two_terms(matrix):
+    high = matrix.astype(jnp.bfloat16)
+    rest = (matrix - high.astype(jnp.float32)).astype(jnp.bfloat16)
+    return jnp.concatenate([high, rest], axis=0)
+
+
 def shifted_taps(tiles, shift, ntaps):
     lane = lax.broadcasted_iota(jnp.int32, tiles[0].shape, 1)
     out = []
@@ -69,10 +77,10 @@
 
 def merge_kernel(
     window, shifts_ref, half_ref, rkern_ref, ukern_ref, angles_ref, taps_ref, x_ref, out_ref,
-    block, outbox, inbox, own_ref, far_ref, send_sem, recv_sem,
+    block, outbox, inbox, own_ref, far_ref, result, send_sem, recv_sem, out_sem,
 ):
-    levels, count = own_ref.shape[0], own_ref.shape[1] // 2
-    phases, ntaps = rkern_ref.shape
+    levels, count = own_ref.shape[0], own_ref.shape[1] // 4
+    ntaps, phases = rkern_ref.shape
     chunks = inbox.shape[1] - 2
     me = lax.axis_index("pulse")
     partners = []
@@ -100,6 +108,10 @@
             device_id_type=MESH,
         )
 
+    def put_out(chunk):
+        columns = pl.ds(pl.multiple_of(chunk * CHUNK, CHUNK), CHUNK)
+        return pltpu.make_async_copy(result.at[chunk], out_ref.at[:, columns], out_sem.at[chunk])
+
     def hand_over(level, chunk, value):
         block[level, chunk + 1] = value
         high = half_ref[level, me] == 0
@@ -123,18 +135,20 @@
         far = shifted_taps(pieces(inbox, level, chunk), shifts_ref[level, partner], ntaps)
         total = jnp.dot(own_ref[level], near, preferred_element_type=jnp.float32)
         total = total + jnp.dot(far_ref[level], far, preferred_element_type=jnp.float32)
-        value = total.astype(jnp.bfloat16)
+        total = total[: 2 * count] + total[2 * count :]
         if level + 1 < levels:
-            hand_over(level + 1, chunk, value)
+            hand_over(level + 1, chunk, total.astype(jnp.bfloat16))
         else:
-            out_ref[:, pl.ds(pl.multiple_of(chunk * CHUNK, CHUNK), CHUNK)] = value
+            result[chunk] = total
+            put_out(chunk).start()
 
     @pl.loop(0, chunks)
     def _(chunk):
         columns = pl.ds(pl.multiple_of(chunk * CHUNK, CHUNK), CHUNK)
         hand_over(0, chunk, x_ref[:, columns])
 
-    base = band_base(ukern_ref, count)
+    base = band_base(ukern_ref[...].astype(jnp.float32), count)
+    rkern = rkern_ref[...]
     for level in range(levels):
         high = half_ref[level, me]
         segments = jnp.where(high == 0, angles_ref[level, :, :count], angles_ref[level, :, count:])
@@ -145,20 +159,23 @@
         weights = [jnp.zeros(phase.shape, jnp.float32)] * ntaps
         for number in range(phases):
             hit = phase == number
-            weights = [jnp.where(hit, rkern_ref[number, t], w) for t, w in enumerate(weights)]
+            weights = [jnp.where(hit, rkern[t : t + 1, number : number + 1], w)
+                for t, w in enumerate(weights)
+           ]
         pad = window - count // 2
         first = pad - high * (count // 2)
         own = level_matrix(base, first, count, here, weights)
-        own_ref[level] = own.astype(jnp.bfloat16)
+        own_ref[level] = two_terms(own)
         far = level_matrix(base, first + high * (count - window), window, there, weights)
-        far_ref[level] = far.astype(jnp.bfloat16)
-
-    last_start = (levels - 1) * GAP
-
-    @pl.loop(0, chunks + 1 + last_start)
+        far_ref[level] = two_terms(far)
+
+    starts = [level * GAP for level in range(levels)]
+    starts[-1] += LAST
+
+    @pl.loop(0, chunks + 1 + starts[-1])
     def _(step):
         for level in range(levels):
-            coming = step - level * GAP
+            coming = step - starts[level]
 
             @pl.when((coming >= 0) & (coming < chunks))
             def _():
@@ -173,6 +190,10 @@
         @pl.loop(0, chunks)
         def _(chunk):
             copy(level, chunk).wait_send()
+
+    @pl.loop(0, chunks)
+    def _(chunk):
+        put_out(chunk).wait()
 
 
 def on_device(beams, ukern, rkern, angles, taps, shifts, half_table):
@@ -184,29 +205,31 @@
     smem = pl.BlockSpec(memory_space=pltpu.SMEM)
     merged = pl.pallas_call(
         functools.partial(merge_kernel, window),
-        out_shape=jax.ShapeDtypeStruct((parts * count, bins), jnp.bfloat16),
-        in_specs=[smem, smem, smem, smem, vmem, vmem, vmem],
-        out_specs=vmem,
+        out_shape=jax.ShapeDtypeStruct((parts * count, bins), jnp.float32),
+        in_specs=[smem, smem, vmem, vmem, vmem, vmem, vmem],
+        out_specs=pl.BlockSpec(memory_space=pl.ANY),
         scratch_shapes=[
             pltpu.VMEM((levels, chunks + 2, parts * count, CHUNK), jnp.bfloat16),
             pltpu.VMEM((levels, chunks, parts * window, CHUNK), jnp.bfloat16),
             pltpu.VMEM((levels, chunks + 2, parts * window, CHUNK), jnp.bfloat16),
-            pltpu.VMEM((levels, parts * count, ntaps * parts * count), jnp.bfloat16),
-            pltpu.VMEM((levels, parts * count, ntaps * parts * window), jnp.bfloat16),
+            pltpu.VMEM((levels, 2 * parts * count, ntaps * parts * count), jnp.bfloat16),
+            pltpu.VMEM((levels, 2 * parts * count, ntaps * parts * window), jnp.bfloat16),
+            pltpu.VMEM((chunks, parts * count, CHUNK), jnp.float32),
             pltpu.SemaphoreType.DMA((levels, chunks)),
             pltpu.SemaphoreType.DMA((levels, chunks)),
+            pltpu.SemaphoreType.DMA((chunks,)),
         ],
         compiler_params=pltpu.CompilerParams(collective_id=0, has_side_effects=True),
     )(
         shifts,
         half_table,
-        rkern,
-        ukern.astype(jnp.float32),
+        rkern.T,
+        ukern,
         angles,
         taps,
         beams.reshape(parts * count, bins),
     )
-    return merged.reshape(parts, count, bins)
+    return merged.astype(jnp.bfloat16).reshape(parts, count, bins)
 
 
 def solution(mesh):

time: 78.3 us -> 60.1 us (0.77)
  Pallas kernels: 73.9 us -> 57.2 us
  local copies, waits for them, and re-layouts: 2.97 us -> 0 us
  other arithmetic: 1.26 us -> 2.69 us
    pallas_call x1, Pallas kernels: 73.9 us -> 57.2 us  [on_device(): pl.pallas_call(functools.partial(merge_kernel, window), out_shape=jax.Sha...]
    unnamed x4 -> x0, local copies, waits for them, and re-layouts: 2.97 us -> none
    convert_element_type x1, other arithmetic: 1.26 us -> 2.69 us  [on_device(): return merged.astype(jnp.bfloat16).reshape(parts, count, bins)]
where the time goes in v3:
time: 60.1 us; the launch traced here: 59.9 us
  Pallas kernels  57.2 us (95%)
  other arithmetic  2.69 us (4%)
    pallas_call x1, Pallas kernels, on_device(): pl.pallas_call(functools.partial(merge_kernel, window), out_shape=jax.Sha...  57.2 us
    convert_element_type x1, other arithmetic, on_device(): return merged.astype(jnp.bfloat16).reshape(parts, count, bins)  2.69 us

profile of v3, /device:TPU:0, one launch (start us, length us, event | category | flops | bytes accessed | tf_op | source)
XLA Modules:
  0.0 59.9 jit_solution(7846486637246049289)
XLA Ops:
  0.0 57.2 %shard_map.73 = f32[128,4096]{1,0:T(8,128)} custom-call(s32[4,16]{1,0:T(4,128)} %shifts_ref.1, s32[4,16]{1,0:T(4,128)} %half_ref.1, f32[4,16]{1,0:T(4,128)} %bitcast.4, bf16[2,32]{1,0:T(2,128)(2,1)} %ukern_ref.1, f32[4,2,128]{2,1,0:T(2,128)} %angles_ref.1, s32[4,64]{1,0:T(4,128)} %taps_ref.1, bf16[128,4096]{1,0:T(8,128)(2,1)} %bitcast.3), custom_call_target="tpu_custom_call" | custom-call | tf_op jit(solution)/shard_map/pallas_call | solution.py:206
  57.2 2.7 %convert_element_type.3 = bf16[128,4096]{1,0:T(8,128)(2,1)} convert(f32[128,4096]{1,0:T(8,128)} %shard_map.73) | non-fusion elementwise | flops 524288 | bytes 3145728 | tf_op jit(solution)/shard_map/convert_element_type | solution.py:232

commit v4 on v3

--- a/solution.py
+++ b/solution.py
@@ -11,6 +11,7 @@
 LANES = 128
 CHUNK = 256
 ROLLED = jnp.bfloat16
+FIRST = 3
 GAP = 3
 LAST = 4
 
@@ -139,7 +140,7 @@
         if level + 1 < levels:
             hand_over(level + 1, chunk, total.astype(jnp.bfloat16))
         else:
-            result[chunk] = total
+            result[chunk] = total.astype(jnp.bfloat16)
             put_out(chunk).start()
 
     @pl.loop(0, chunks)
@@ -149,7 +150,7 @@
 
     base = band_base(ukern_ref[...].astype(jnp.float32), count)
     rkern = rkern_ref[...]
-    for level in range(levels):
+    def build(level):
         high = half_ref[level, me]
         segments = jnp.where(high == 0, angles_ref[level, :, :count], angles_ref[level, :, count:])
         upper = lax.rem(me // 2**level, 2) == 1
@@ -169,13 +170,17 @@
         far = level_matrix(base, first + high * (count - window), window, there, weights)
         far_ref[level] = two_terms(far)
 
-    starts = [level * GAP for level in range(levels)]
+    starts = [0] + [FIRST + level * GAP for level in range(levels - 1)]
     starts[-1] += LAST
 
     @pl.loop(0, chunks + 1 + starts[-1])
     def _(step):
         for level in range(levels):
             coming = step - starts[level]
+
+            @pl.when(coming == 0)
+            def _():
+                build(level)
 
             @pl.when((coming >= 0) & (coming < chunks))
             def _():
@@ -205,7 +210,7 @@
     smem = pl.BlockSpec(memory_space=pltpu.SMEM)
     merged = pl.pallas_call(
         functools.partial(merge_kernel, window),
-        out_shape=jax.ShapeDtypeStruct((parts * count, bins), jnp.float32),
+        out_shape=jax.ShapeDtypeStruct((parts * count, bins), jnp.bfloat16),
         in_specs=[smem, smem, vmem, vmem, vmem, vmem, vmem],
         out_specs=pl.BlockSpec(memory_space=pl.ANY),
         scratch_shapes=[
@@ -214,7 +219,7 @@
             pltpu.VMEM((levels, chunks + 2, parts * window, CHUNK), jnp.bfloat16),
             pltpu.VMEM((levels, 2 * parts * count, ntaps * parts * count), jnp.bfloat16),
             pltpu.VMEM((levels, 2 * parts * count, ntaps * parts * window), jnp.bfloat16),
-            pltpu.VMEM((chunks, parts * count, CHUNK), jnp.float32),
+            pltpu.VMEM((chunks, parts * count, CHUNK), jnp.bfloat16),
             pltpu.SemaphoreType.DMA((levels, chunks)),
             pltpu.SemaphoreType.DMA((levels, chunks)),
             pltpu.SemaphoreType.DMA((chunks,)),
@@ -229,7 +234,7 @@
         taps,
         beams.reshape(parts * count, bins),
     )
-    return merged.astype(jnp.bfloat16).reshape(parts, count, bins)
+    return merged.reshape(parts, count, bins)
 
 
 def solution(mesh):

time: 60.1 us -> 57.7 us (0.960)
  other arithmetic: 2.69 us -> 0 us
  local copies, waits for them, and re-layouts: 0 us -> 2.29 us
  Pallas kernels: 57.2 us -> 55.2 us
    convert_element_type x1 -> x0, other arithmetic: 2.69 us -> none  [on_device(): return merged.astype(jnp.bfloat16).reshape(parts, count, bins)]
    unnamed x0 -> x1, local copies, waits for them, and re-layouts: none -> 2.29 us
    pallas_call x1, Pallas kernels: 57.2 us -> 55.2 us  [on_device(): pl.pallas_call(functools.partial(merge_kernel, window), out_shape=jax.Sha...]
where the time goes in v4:
time: 57.7 us; the launch traced here: 57.5 us
  Pallas kernels  55.2 us (96%)
  local copies, waits for them, and re-layouts  2.29 us (4%)
    pallas_call x1, Pallas kernels, on_device(): pl.pallas_call(functools.partial(merge_kernel, window), out_shape=jax.Sha...  55.2 us
    unnamed x1, local copies, waits for them, and re-layouts  2.29 us

profile of v4, /device:TPU:0, one launch (start us, length us, event | category | flops | bytes accessed | tf_op | source)
XLA Modules:
  0.0 57.5 jit_solution(7774558841466148123)
XLA Ops:
  0.0 55.2 %shard_map.73 = bf16[128,4096]{1,0:T(8,128)(2,1)} custom-call(s32[4,16]{1,0:T(4,128)} %shifts_ref.1, s32[4,16]{1,0:T(4,128)} %half_ref.1, f32[4,16]{1,0:T(4,128)} %bitcast.5, bf16[2,32]{1,0:T(2,128)(2,1)} %ukern_ref.1, f32[4,2,128]{2,1,0:T(2,128)} %angles_ref.1, s32[4,64]{1,0:T(4,128)} %taps_ref.1, bf16[128,4096]{1,0:T(8,128)(2,1)} %bitcast.4), custom_call_target="tpu_custom_call" | custom-call | tf_op jit(solution)/shard_map/pallas_call | solution.py:211
  55.2 2.3 %copy.9 = bf16[2,64,4096]{2,1,0:T(8,128)(2,1)} copy(bf16[2,64,4096]{2,1,0:T(8,128)(2,1)} %bitcast.3) | data formatting | bytes 2097152

commit v5 on v4

--- a/solution.py
+++ b/solution.py
@@ -11,9 +11,9 @@
 LANES = 128
 CHUNK = 256
 ROLLED = jnp.bfloat16
-FIRST = 3
+FIRST = 4
 GAP = 3
-LAST = 4
+LAST = 6
 
 
 def band_base(ukern, count):

time: 57.7 us -> 57.6 us (level)
  no operation moved by 1% of the time
where the time goes in v5:
time: 57.6 us; the launch traced here: 57.5 us
  Pallas kernels  55.2 us (96%)
  local copies, waits for them, and re-layouts  2.29 us (4%)
    pallas_call x1, Pallas kernels, on_device(): pl.pallas_call(functools.partial(merge_kernel, window), out_shape=jax.Sha...  55.2 us
    unnamed x1, local copies, waits for them, and re-layouts  2.29 us

profile of v5, /device:TPU:0, one launch (start us, length us, event | category | flops | bytes accessed | tf_op | source)
XLA Modules:
  0.0 57.5 jit_solution(7000582208252572178)
XLA Ops:
  0.0 55.2 %shard_map.73 = bf16[128,4096]{1,0:T(8,128)(2,1)} custom-call(s32[4,16]{1,0:T(4,128)} %shifts_ref.1, s32[4,16]{1,0:T(4,128)} %half_ref.1, f32[4,16]{1,0:T(4,128)} %bitcast.5, bf16[2,32]{1,0:T(2,128)(2,1)} %ukern_ref.1, f32[4,2,128]{2,1,0:T(2,128)} %angles_ref.1, s32[4,64]{1,0:T(4,128)} %taps_ref.1, bf16[128,4096]{1,0:T(8,128)(2,1)} %bitcast.4), custom_call_target="tpu_custom_call" | custom-call | tf_op jit(solution)/shard_map/pallas_call | solution.py:211
  55.2 2.3 %copy.9 = bf16[2,64,4096]{2,1,0:T(8,128)(2,1)} copy(bf16[2,64,4096]{2,1,0:T(8,128)(2,1)} %bitcast.3) | data formatting | bytes 2097152
